TPU v7x, 256 devices: a whole 4x4x8 slice. The times are simulated.
256 devices in a mesh: grp: 4 (over y), own: 64 (over x, z, core).
Axes of the slice: x: 4, y: 4, z: 8, core: 2. Of those that a mesh axis runs over, the one named last changes fastest.
Arguments:
- arrivals: bfloat16 [131072, 512], P(('grp', 'own')), may hold values from -6 to 6
- home_owner: int32 [131072, 1], P(('grp', 'own')), may hold values from 0 to 63; in each aligned block of 512 rows (0 to 511, 512 to 1023, ...) at most 16 rows name the same one
- cluster_slot: int32 [131072], P(('grp', 'own')), may hold values from 0 to 255
- bank: bfloat16 [16384, 32, 512], P('own'), may hold values from -6 to 6
- members: int32 [16384], P('own'), may hold values from 1 to 32
- centroid_sum: float32 [16384, 512], P('own'), may hold values from -1.6 to 1.6
Outputs:
- best_cosine: float32 [131072], P(('grp', 'own'))
- centroids: float32 [16384, 512], P('own')
Inputs may be any that keep to these rules, and one draw needn't show every extreme that they name: `home_owner`: among the 512 rows of one device no value appears more than 16 times, and some value appears exactly 16 times.
All inputs are finite; a program needn't handle non-finite values.
Results may differ from a plain program's by a relative error of at most 0.0017.
Values may be sent and summed in bfloat16 or wider, within the bound.
A program may use at most 64 MiB of HBM per device.

v0:
```python
import jax
import jax.numpy as jnp
from jax import lax
from jax.sharding import PartitionSpec as P

epsilon = 1e-06


def normalize_rows(total):
    return total / jnp.sqrt(jnp.sum(total * total, axis=1, keepdims=True) + epsilon)


def body(arrivals, home_owner, cluster_slot, bank, members, centroid_sum):
    owners = lax.axis_size("own")
    local_rows = arrivals.shape[0]
    width = arrivals.shape[1]
    local_clusters = bank.shape[0]
    block_depth = bank.shape[1]
    capacity = 2 * local_rows // owners
    total_slots = owners * capacity
    values = arrivals.astype(jnp.float32)
    unit_rows = (
        values / jnp.sqrt(jnp.sum(values * values, axis=1, keepdims=True) + epsilon)
    ).astype(jnp.bfloat16)
    target = home_owner[:, 0]
    target_hit = target[:, None] == jnp.arange(owners, dtype=jnp.int32)[None, :]
    row_iota = jnp.arange(local_rows, dtype=jnp.int32)
    strictly_below = (row_iota[:, None] > row_iota[None, :]).astype(jnp.bfloat16)
    earlier = jnp.dot(
        strictly_below, target_hit.astype(jnp.bfloat16), preferred_element_type=jnp.float32
    )
    placed = jnp.sum(jnp.where(target_hit, earlier, 0.0), axis=1).astype(jnp.int32)
    slot_index = target * capacity + placed
    slot_iota = jnp.arange(total_slots, dtype=jnp.int32)
    slot_match = slot_iota[:, None] == slot_index[None, :]
    send_rows = (
        jnp.dot(slot_match.astype(jnp.bfloat16), unit_rows, preferred_element_type=jnp.float32)
        .astype(jnp.bfloat16)
        .reshape(owners, capacity, width)
    )
    send_slot = (jnp.sum(jnp.where(slot_match, cluster_slot[None, :] + 1, 0), axis=1) - 1).reshape(
        owners, capacity
    )
    bank_flat = bank.reshape(local_clusters * block_depth, width)
    bank_norm = jnp.sqrt(
        jnp.einsum("rd,rd->r", bank_flat, bank_flat, preferred_element_type=jnp.float32) + epsilon
    )
    column_cluster = jnp.arange(local_clusters * block_depth, dtype=jnp.int32) // block_depth
    column_depth = jnp.arange(local_clusters * block_depth, dtype=jnp.int32) % block_depth
    member_hit = (
        jnp.arange(local_clusters, dtype=jnp.int32)[:, None] == column_cluster[None, :]
    ).astype(jnp.int32)
    column_members = jnp.sum(member_hit * members[:, None], axis=0)
    column_live = column_depth < column_members
    column_code = jnp.where(column_live, column_cluster, -2)

    def score_tile(query, chosen):
        dot_raw = lax.dot_general(
            query, bank_flat, (((1,), (1,)), ((), ())), preferred_element_type=jnp.float32
        )
        cosine = dot_raw / bank_norm[None, :]
        is_valid = column_code[None, :] == chosen[:, None]
        return jnp.max(jnp.where(is_valid, cosine, -3.0), axis=1)

    got_rows, got_slot = (
        lax.all_to_all(send_rows, "own", split_axis=0, concat_axis=0, tiled=True),
        lax.all_to_all(send_slot, "own", split_axis=0, concat_axis=0, tiled=True),
    )
    flat_rows = got_rows.reshape(total_slots, width)
    flat_slot = got_slot.reshape(total_slots)
    count = flat_rows.shape[0]
    tile = min(256, count)
    tiles = count // tile

    def mapped_tile(inputs):
        return score_tile(inputs[0], inputs[1])

    flat_best = lax.map(
        mapped_tile, (flat_rows.reshape(tiles, tile, width), flat_slot.reshape(tiles, tile))
    ).reshape(count)
    returned = lax.all_to_all(
        flat_best.reshape(owners, capacity), "own", split_axis=0, concat_axis=0, tiled=True
    )
    best_cosine = jnp.sum(
        jnp.where(slot_match, returned.reshape(total_slots)[:, None], 0.0), axis=0
    )
    cluster_hit = (
        jnp.arange(local_clusters, dtype=jnp.int32)[:, None] == flat_slot[None, :]
    ).astype(jnp.bfloat16)
    partial_value = jnp.dot(cluster_hit, flat_rows, preferred_element_type=jnp.float32)
    summed = lax.psum(partial_value, "grp")
    centroids = normalize_rows(centroid_sum + summed)
    return (best_cosine, centroids)


def solution(mesh):
    return jax.shard_map(
        body,
        mesh=mesh,
        in_specs=(
            P(("grp", "own"), None),
            P(("grp", "own"), None),
            P(("grp", "own")),
            P("own", None, None),
            P("own"),
            P("own", None),
        ),
        out_specs=(P(("grp", "own")), P("own", None)),
        check_vma=False,
    )
```

profile of v0, /device:TPU:8, one launch (start us, length us, event | category | flops | bytes accessed | tf_op | source)
XLA Modules:
  0.0 119.7 jit_solution(3658377134532595293)
XLA Ops:
  7.2 1.0 fusion.6
  8.2 0.7 convert_add_fusion
  9.2 0.7 sub.16
  9.9 11.9 %all-to-all-start = ((s32[64,1,16]{2,1,0:T(1,128)}), s32[64,1,16]{2,1,0:T(1,128)S(1)}, u32[]{:S(2)}, u32[]{:S(2)}) async-start(s32[64,1,16]{2,1,0:T(1,128)} %bitcast.4), calls=%async_computation | async-start | bytes 65536 | tf_op jit(solution)/shard_map/all_to_all | solution.py:67
  21.9 1.2 %fusion.7 = f32[512]{0:T(512)S(1)} fusion(bf16[512,512]{1,0:T(8,128)(2,1)} %param.8), kind=kLoop, calls=%fused_computation.18 | loop fusion | flops 785920 | bytes 526336 | tf_op jit(solution)/shard_map/reduce_sum | solution.py:23
  23.1 2.8 %fusion.5 = bf16[1024,512]{1,0:T(8,128)(2,1)} fusion(s32[512]{0:T(512)S(1)} %get-tuple-element.56, bf16[512,512]{1,0:T(8,128)(2,1)} %param.8, f32[512]{0:T(512)S(1)} %add_sqrt_fusion.1), kind=kOutput, calls=%fused_computation.13 | convolution fusion | flops 538705920 | bytes 1576960 | tf_op jit(solution)/shard_map/dot_general | solution.py:37
  25.9 5.4 %all-to-all-done = s32[64,1,16]{2,1,0:T(1,128)S(1)} async-done(((s32[64,1,16]{2,1,0:T(1,128)}), s32[64,1,16]{2,1,0:T(1,128)S(1)}, u32[]{:S(2)}, u32[]{:S(2)}) %all-to-all-start) | async-done | bytes 4128 | tf_op jit(solution)/shard_map/all_to_all | solution.py:67
  31.3 5.0 %all-to-all-start.1 = ((bf16[64,16,512]{2,1,0:T(8,128)(2,1)}), bf16[64,16,512]{2,1,0:T(8,128)(2,1)S(1)}, u32[]{:S(2)}, u32[]{:S(2)}) async-start(bf16[64,16,512]{2,1,0:T(8,128)(2,1)} %bitcast.5), calls=%async_computation.1 | async-start | bytes 2097152 | tf_op jit(solution)/shard_map/all_to_all | solution.py:66
  36.4 1.4 %select_reduce_fusion.1 = s32[8192]{0:T(1024)S(1)} fusion(s32[256]{0:T(256)S(1)} %copy-done.1, s32[8192]{0:T(1024)S(1)} %add_select_fusion), kind=kLoop, calls=%fused_computation.7 | loop fusion | flops 6283264 | bytes 66560 | tf_op jit(solution)/shard_map/reduce_sum | solution.py:53
  37.8 5.1 %fusion.3 = f32[8192]{0:T(1024)S(1)} fusion(bf16[256,32,512]{2,1,0:T(8,128)(2,1)} %param.11), kind=kLoop, calls=%fused_computation.6 | loop fusion | flops 12574720 | bytes 8421376 | tf_op jit(solution)/shard_map/rd,rd->r/dot_general | solution.py:46
  43.5 0.7 reduce.10
  44.3 20.1 %all-to-all-done.1 = bf16[64,16,512]{2,1,0:T(8,128)(2,1)S(1)} async-done(((bf16[64,16,512]{2,1,0:T(8,128)(2,1)}), bf16[64,16,512]{2,1,0:T(8,128)(2,1)S(1)}, u32[]{:S(2)}, u32[]{:S(2)}) %all-to-all-start.1) | async-done | bytes 1048608 | tf_op jit(solution)/shard_map/all_to_all | solution.py:66
  64.4 1.2 %fusion.10 = f32[256,512]{1,0:T(8,128)} fusion(bf16[1024,512]{1,0:T(8,128)(2,1)S(1)} %bitcast.25, s32[1024]{0:T(1024)S(1)} %eq.81), kind=kOutput, calls=%fused_computation.23 | convolution fusion | flops 268697600 | bytes 1576960 | tf_op jit(solution)/shard_map/dot_general | solution.py:90
  65.7 24.2 %while.10 = (s32[]{:T(128)}, f32[4,256]{1,0:T(4,128)S(1)}, s32[8192]{0:T(1024)S(1)}, s32[4,256]{1,0:T(4,128)S(1)}, bf16[4,256,512]{2,1,0:T(8,128)(2,1)S(1)}, /*i...) while((s32[]{:T(128)}, f32[4,256]{1,0:T(4,128)S(1)}, s32[8192]{0:T(1024)S(1)}, ...), condition=%wide.region_6.7_spmd, body=%wide.region_4.6_spmd.sunk | while | flops 2155872000 | bytes 8722537 | solution.py:78
  65.7 6.0 %select_reduce_fusion.5 = f32[256]{0:T(256)S(1)} fusion(bf16[8192,512]{1,0:T(8,128)(2,1)} %get-tuple-element.124, f32[8192]{0:T(1024)S(1)} %get-tuple-element.125, s32[8192]{0:T(1024)S(1)} %get-tuple-element.121, s32[256]{0:T(256)S(1)} %bitcast.30, bf16[4,256,512]{2,1,0:T(8,128)(2,1)S(1)} %get-tuple-element.123, s32[]{:T(128)} %get-tuple-element.110), kind=kOutput, calls=%fused_computation.clone.1 | convolution fusion | flops 2155872000 | bytes 8718340 | tf_op jit(solution)/shard_map/while/body/eval_jaxpr/dot_general | solution.py:58
  71.8 6.0 %select_reduce_fusion.5 = f32[256]{0:T(256)S(1)} fusion(bf16[8192,512]{1,0:T(8,128)(2,1)} %get-tuple-element.124, f32[8192]{0:T(1024)S(1)} %get-tuple-element.125, s32[8192]{0:T(1024)S(1)} %get-tuple-element.121, s32[256]{0:T(256)S(1)} %bitcast.30, bf16[4,256,512]{2,1,0:T(8,128)(2,1)S(1)} %get-tuple-element.123, s32[]{:T(128)} %get-tuple-element.110), kind=kOutput, calls=%fused_computation.clone.1 | convolution fusion | flops 2155872000 | bytes 8718340 | tf_op jit(solution)/shard_map/while/body/eval_jaxpr/dot_general | solution.py:58
  77.9 6.0 %select_reduce_fusion.5 = f32[256]{0:T(256)S(1)} fusion(bf16[8192,512]{1,0:T(8,128)(2,1)} %get-tuple-element.124, f32[8192]{0:T(1024)S(1)} %get-tuple-element.125, s32[8192]{0:T(1024)S(1)} %get-tuple-element.121, s32[256]{0:T(256)S(1)} %bitcast.30, bf16[4,256,512]{2,1,0:T(8,128)(2,1)S(1)} %get-tuple-element.123, s32[]{:T(128)} %get-tuple-element.110), kind=kOutput, calls=%fused_computation.clone.1 | convolution fusion | flops 2155872000 | bytes 8718340 | tf_op jit(solution)/shard_map/while/body/eval_jaxpr/dot_general | solution.py:58
  83.9 6.0 %select_reduce_fusion.5 = f32[256]{0:T(256)S(1)} fusion(bf16[8192,512]{1,0:T(8,128)(2,1)} %get-tuple-element.124, f32[8192]{0:T(1024)S(1)} %get-tuple-element.125, s32[8192]{0:T(1024)S(1)} %get-tuple-element.121, s32[256]{0:T(256)S(1)} %bitcast.30, bf16[4,256,512]{2,1,0:T(8,128)(2,1)S(1)} %get-tuple-element.123, s32[]{:T(128)} %get-tuple-element.110), kind=kOutput, calls=%fused_computation.clone.1 | convolution fusion | flops 2155872000 | bytes 8718340 | tf_op jit(solution)/shard_map/while/body/eval_jaxpr/dot_general | solution.py:58
  90.0 15.9 %all_to_all.20 = f32[64,1,16]{2,1,0:T(1,128)S(1)} all-to-all(f32[64,1,16]{2,1,0:T(1,128)S(1)} %bitcast.28), channel_id=1, replica_groups=mesh['grp'=4,'own'=64] {'own'}, dimensions={0} | all-to-all | bytes 8192 | tf_op jit(solution)/shard_map/all_to_all | solution.py:81
  106.4 0.7 reduce.11
  107.2 0.9 select_reduce_fusion.2
  108.1 2.6 %all-reduce.2.cloned.1.call-done = f32[256,512]{1,0:T(8,128)} async-done(((f32[256,512]{1,0:T(8,128)}), f32[256,512]{1,0:T(8,128)}) %all-reduce.2.cloned.1.call-update) | async-done | bytes 524304 | tf_op jit(solution)/shard_map/psum | solution.py:91
  110.7 1.2 multiply_reduce_fusion
  111.9 0.9 broadcast_divide_fusion
  (28 shorter events, 1.9 us)
Async XLA Ops:
  7.2 29.2 %copy-start.1 = (s32[256]{0:T(256)S(1)}, s32[256]{0:T(256)}, u32[]{:S(2)}) copy-start(s32[256]{0:T(256)} %param.12) | copy-start | bytes 3076
  9.9 21.4 %all-to-all-start = ((s32[64,1,16]{2,1,0:T(1,128)}), s32[64,1,16]{2,1,0:T(1,128)S(1)}, u32[]{:S(2)}, u32[]{:S(2)}) async-start(s32[64,1,16]{2,1,0:T(1,128)} %bitcast.4), calls=%async_computation | async-start | bytes 65536 | tf_op jit(solution)/shard_map/all_to_all | solution.py:67
  31.3 33.1 %all-to-all-start.1 = ((bf16[64,16,512]{2,1,0:T(8,128)(2,1)}), bf16[64,16,512]{2,1,0:T(8,128)(2,1)S(1)}, u32[]{:S(2)}, u32[]{:S(2)}) async-start(bf16[64,16,512]{2,1,0:T(8,128)(2,1)} %bitcast.5), calls=%async_computation.1 | async-start | bytes 2097152 | tf_op jit(solution)/shard_map/all_to_all | solution.py:66
  36.3 74.4 %all-reduce.2.cloned.1.call-start = ((), (), s32[]{:S(2)}) async-start(), calls=%async_computation.3 | async-start | bytes 1048576 | tf_op jit(solution)/shard_map/psum | solution.py:91
  65.7 45.0 %copy-start = (f32[256,512]{1,0:T(8,128)S(1)}, f32[256,512]{1,0:T(8,128)}, u32[]{:S(2)}) copy-start(f32[256,512]{1,0:T(8,128)} %param.13) | copy-start | bytes 1572868
Sparse Core Ops, SparseCore 0:
  65.8 44.8 all-reduce.1
where the time goes:
time: 121 us; the launch traced here: 120 us
  matrix products  29.1 us (24%)
  waiting for transfers between devices  28.1 us (23%)
  starting transfers between devices  16.9 us (14%)
  blocking collectives  15.9 us (13%)
  between operations  14.2 us (12%)
  other arithmetic  13.2 us (11%)
  local copies, waits for them, and re-layouts  2.23 us (2%)
    dot_general x4, matrix products, score_tile(): lax.dot_general(query, bank_flat, (((1,), (1,)), ((), ())), preferred_ele...  24 us
    all_to_all x1, waiting for transfers between devices, body(): lax.all_to_all(send_rows, 'own', split_axis=0, concat_axis=0, tiled=True)  20.1 us
    all_to_all x1, blocking collectives, body(): lax.all_to_all(flat_best.reshape(owners, capacity), 'own', split_axis=0,...  15.9 us
    all_to_all x1, starting transfers between devices, body(): lax.all_to_all(send_slot, 'own', split_axis=0, concat_axis=0, tiled=True)  11.9 us
    all_to_all x1, waiting for transfers between devices, body(): lax.all_to_all(send_slot, 'own', split_axis=0, concat_axis=0, tiled=True)  5.37 us
    dot_general x1, other arithmetic, body(): jnp.einsum('rd,rd->r', bank_flat, bank_flat, preferred_element_type=jnp.f...  5.11 us
    all_to_all x1, starting transfers between devices, body(): lax.all_to_all(send_rows, 'own', split_axis=0, concat_axis=0, tiled=True)  4.95 us
    dot_general x1, matrix products, body(): jnp.dot(slot_match.astype(jnp.bfloat16), unit_rows, preferred_element_typ...  2.85 us
  transfers between devices with their start and end apart: 3, of which 3 were waited for; matrix products, arithmetic and copies ran while one was open for 32% of the time, Pallas kernels for 0%

commit v1 on v0

v1 whole, which is shorter than its diff:
```python
import functools

import jax
import jax.numpy as jnp
from jax import lax
from jax.experimental import pallas as pl
from jax.experimental.pallas import tpu as pltpu
from jax.sharding import PartitionSpec as P

EPS = 1e-06
MESH = pl.DeviceIdType.MESH
Z_ORDER = (4, 0, 3, 5, 2, 6, 1, 7)
SELF_GROUP = Z_ORDER.index(0)
F32, BF16 = jnp.float32, jnp.bfloat16
TILE = 512


def nt(a, b):
    return lax.dot_general(a, b, (((1,), (1,)), ((), ())), preferred_element_type=F32)


def peer(x, z, c, dz, q, sign):
    dx, dc = q // 2, q % 2
    px = lax.rem(x + sign * dx + 4, 4)
    pz = lax.rem(z + sign * dz + 8, 8)
    pc = lax.rem(c + dc, 2)
    return px * 16 + pz * 2 + pc


def kernel(
    arr_h, tgt, slot, bank_h, mem, csum_h, best_o, cent_o,
    arr, bank, rn, colc, kbuf, send, recv, scode, rcode, bests, ret, r8,
    acc, csum, rs_out, rs_in, ag,
    in_sem, bank_sem, self_sem, row_ss, row_rs, code_ss, code_rs, ret_ss, ret_rs,
    rs_ss, rs_rs, ag_ss, ag_rs,
):
    g = lax.axis_index("grp")
    me = lax.axis_index("own")
    x, z, c = me // 16, lax.rem(me // 2, 8), lax.rem(me, 2)
    clusters = mem.shape[0]
    quarter = clusters // 4

    arr_cp = pltpu.make_async_copy(arr_h, arr, in_sem.at[0])
    arr_cp.start()
    csum_cp = pltpu.make_async_copy(
        csum_h.at[pl.ds(g * quarter, quarter), :], csum, in_sem.at[1]
    )
    csum_cp.start()
    bank_cp = pltpu.make_async_copy(bank_h, bank, bank_sem)
    bank_cp.start()

    barrier = pltpu.get_barrier_semaphore()
    for zi, dz in enumerate(Z_ORDER):
        @pl.loop(1 if zi == SELF_GROUP else 0, 8)
        def _(q):
            pl.semaphore_signal(
                barrier, inc=1, device_id=(g, peer(x, z, c, dz, q, 1)), device_id_type=MESH
            )
    for j in range(1, 4):
        pl.semaphore_signal(
            barrier, inc=1, device_id=(lax.rem(g + j, 4), me), device_id_type=MESH
        )

    t = tgt[...]
    dx = ((t >> 4) - x) & 3
    dz = ((t >> 1) - z) & 7
    dc = (t - c) & 1
    zi_of = jnp.zeros_like(t)
    for zi, d in enumerate(Z_ORDER):
        zi_of = jnp.where(dz == d, zi, zi_of)
    pos = zi_of * 8 + dx * 2 + dc
    rows = t.shape[1]
    hit = lax.broadcasted_iota(jnp.int32, (64, rows), 0) == pos
    upper = (
        lax.broadcasted_iota(jnp.int32, (rows, rows), 0)
        < lax.broadcasted_iota(jnp.int32, (rows, rows), 1)
    ).astype(F32).astype(BF16)
    earlier = jnp.dot(hit.astype(F32).astype(BF16), upper, preferred_element_type=F32)
    placed = jnp.sum(jnp.where(hit, earlier, 0.0), axis=0, keepdims=True).astype(jnp.int32)
    k = pos * 16 + placed
    kbuf[...] = k
    code_row = jnp.broadcast_to((slot[...] + 1).astype(F32), (8, rows)).astype(BF16)

    arr_cp.wait()
    values = arr[...].astype(F32)
    unit = (
        values / jnp.sqrt(jnp.sum(values * values, axis=1, keepdims=True) + EPS)
    ).astype(BF16)
    iota128 = lax.broadcasted_iota(jnp.int32, (128, rows), 0)
    for zi in range(8):
        match = (iota128 + zi * 128 == k).astype(F32).astype(BF16)
        send[pl.ds(zi * 8, 8)] = (
            jnp.dot(match, unit, preferred_element_type=F32).astype(BF16).reshape(8, 16, -1)
        )
        scode[zi] = nt(code_row, match)[0:1, :] - 1.0

    pl.semaphore_wait(barrier, 66)

    def row_copy(zi, lo, n, dev):
        part = pl.ds(zi * 8 + lo, n)
        return pltpu.make_async_remote_copy(
            src_ref=send.at[part], dst_ref=recv.at[part], send_sem=row_ss.at[zi],
            recv_sem=row_rs.at[zi], device_id=(g, dev), device_id_type=MESH,
        )

    def code_copy(zi, q, dev):
        return pltpu.make_async_remote_copy(
            src_ref=scode.at[zi], dst_ref=rcode.at[zi * 8 + q], send_sem=code_ss.at[zi],
            recv_sem=code_rs.at[zi], device_id=(g, dev), device_id_type=MESH,
        )

    def ret_copy(zi, q, dev):
        return pltpu.make_async_remote_copy(
            src_ref=bests.at[zi], dst_ref=ret.at[zi * 8 + q], send_sem=ret_ss.at[zi],
            recv_sem=ret_rs.at[zi], device_id=(g, dev), device_id_type=MESH,
        )

    def landed(buf, zi, sem):
        lo = 1 if zi == SELF_GROUP else 0
        part = pl.ds(zi * 8 + lo, 8 - lo)
        return pltpu.make_async_remote_copy(
            src_ref=buf.at[part], dst_ref=buf.at[part], send_sem=sem.at[zi],
            recv_sem=sem.at[zi], device_id=(g, me), device_id_type=MESH,
        )

    me_slot = SELF_GROUP * 8
    self_cp = pltpu.make_async_copy(send.at[me_slot], recv.at[me_slot], self_sem)
    self_cp.start()
    rcode[me_slot] = scode[SELF_GROUP]
    for chunk in range(4):
        @pl.loop(0, 8)
        def _(q):
            for zi in (2 * chunk, 2 * chunk + 1):
                if zi != SELF_GROUP:
                    dev = peer(x, z, c, Z_ORDER[zi], q, 1)
                    code_copy(zi, q, dev).start()
                    row_copy(zi, q, 1, dev).start()
        if SELF_GROUP // 2 == chunk:
            @pl.loop(1, 8)
            def _(q):
                dev = peer(x, z, c, 0, q, 1)
                code_copy(SELF_GROUP, q, dev).start()
                row_copy(SELF_GROUP, q, 1, dev).start()

    @pl.loop(0, clusters)
    def _(cl):
        live = lax.broadcasted_iota(jnp.int32, (32, 128), 0) < mem[cl]
        colc[pl.ds(pl.multiple_of(cl * 32, 32), 32), :] = jnp.where(
            live, jnp.full((32, 128), cl, jnp.int32), -2
        ).astype(F32)

    bank_cp.wait()

    @pl.loop(0, bank.shape[0] // 256)
    def _(i):
        part = pl.ds(pl.multiple_of(i * 256, 256), 256)
        b = bank[part, :].astype(F32)
        norm = 1.0 / jnp.sqrt(jnp.sum(b * b, axis=1, keepdims=True) + EPS)
        rn[part, :] = jnp.broadcast_to(norm, (256, 128))

    lane16 = lax.broadcasted_iota(jnp.int32, (1, 128), 1) // 16

    def folded(buf, zi):
        total = jnp.zeros((1, 128), F32)
        for q in range(8):
            total = jnp.where(lane16 == q, buf[zi * 8 + q], total)
        return total

    def self_lo(zi):
        return 1 if zi == SELF_GROUP else 0

    acc[...] = jnp.zeros_like(acc)
    for chunk in range(4):
        for zi in (2 * chunk, 2 * chunk + 1):
            lo = self_lo(zi)
            landed(recv, zi, row_rs).wait_recv()
            landed(rcode, zi, code_rs).wait_recv()
            if lo:
                self_cp.wait()
        codes = [folded(rcode, zi) for zi in (2 * chunk, 2 * chunk + 1)]
        q_rows = recv[pl.ds(chunk * 16, 16)].reshape(256, -1)
        row_of = jnp.concatenate(codes, axis=1)
        which = (
            lax.broadcasted_iota(jnp.int32, (clusters, 256), 0).astype(F32) == row_of
        ).astype(F32).astype(BF16)
        acc[...] += jnp.dot(which, q_rows, preferred_element_type=F32)
        if chunk == 3:
            for j in range(1, 4):
                to = lax.rem(g + j, 4)
                rs_out[j - 1] = acc[pl.ds(to * quarter, quarter), :]
                rs_copy(g, me, j, rs_out, rs_in, rs_ss, rs_rs).start()

        def tile(i, best):
            part = pl.ds(pl.multiple_of(i * TILE, TILE), TILE)
            s = nt(bank[part, :], q_rows)
            scale, cols = rn[part, :], colc[part, :]
            new = []
            for h in range(2):
                cand = jnp.where(
                    cols == codes[h], s[:, h * 128 : h * 128 + 128] * scale, -3.0
                ).reshape(TILE // 8, 8, 128)
                new.append(jnp.maximum(best[h], jnp.max(cand, axis=0)))
            return tuple(new)

        start = jnp.full((8, 128), -3.0, F32)
        best = lax.fori_loop(0, bank.shape[0] // TILE, tile, (start, start))
        for h in range(2):
            zi = 2 * chunk + h
            bests[zi] = jnp.max(best[h], axis=0, keepdims=True)
            if zi == SELF_GROUP:
                ret[me_slot] = bests[zi]

            @pl.loop(self_lo(zi), 8)
            def _(q):
                ret_copy(zi, q, peer(x, z, c, Z_ORDER[zi], q, -1)).start()

    csum_cp.wait()
    total = csum[...] + acc[pl.ds(g * quarter, quarter), :]
    for j in range(1, 4):
        rs_copy(g, me, j, rs_out, rs_in, rs_ss, rs_rs).wait_recv()
        total += rs_in[j - 1]
    ag[g] = total / jnp.sqrt(jnp.sum(total * total, axis=1, keepdims=True) + EPS)
    for j in range(1, 4):
        ag_copy(g, me, j, ag, ag_ss, ag_rs, g).start()

    for zi in range(8):
        landed(ret, zi, ret_rs).wait_recv()
    for zi in range(8):
        r8[zi : zi + 1, :] = folded(ret, zi)
    k = kbuf[...]
    group = (lax.broadcasted_iota(jnp.int32, (8, rows), 0) == (k >> 7)).astype(F32)
    spread = lax.dot_general(
        r8[...], group, (((0,), (0,)), ((), ())),
        preferred_element_type=F32, precision=lax.Precision.HIGHEST,
    )
    best_o[...] = jnp.sum(
        jnp.where(iota128 == (k & 127), spread, 0.0), axis=0, keepdims=True
    )

    for j in range(1, 4):
        ag_copy(g, me, j, ag, ag_ss, ag_rs, lax.rem(g + 4 - j, 4)).wait_recv()
    cent_o[...] = ag[...].reshape(clusters, -1)

    for zi in range(8):
        landed(send, zi, row_ss).wait_send()
        landed(rcode, zi, code_ss).wait_send()
        landed(ret, zi, ret_ss).wait_send()
    for j in range(1, 4):
        rs_copy(g, me, j, rs_out, rs_in, rs_ss, rs_rs).wait_send()
        ag_copy(g, me, j, ag, ag_ss, ag_rs, g).wait_send()


def rs_copy(g, me, j, rs_out, rs_in, ss, rs):
    return pltpu.make_async_remote_copy(
        src_ref=rs_out.at[j - 1], dst_ref=rs_in.at[j - 1], send_sem=ss.at[j - 1],
        recv_sem=rs.at[j - 1], device_id=(lax.rem(g + j, 4), me), device_id_type=MESH,
    )


def ag_copy(g, me, j, ag, ss, rs, at):
    return pltpu.make_async_remote_copy(
        src_ref=ag.at[at], dst_ref=ag.at[at], send_sem=ss.at[j - 1],
        recv_sem=rs.at[j - 1], device_id=(lax.rem(g + j, 4), me), device_id_type=MESH,
    )


def body(arrivals, home_owner, cluster_slot, bank, members, centroid_sum):
    rows, width = arrivals.shape
    clusters, depth, _ = bank.shape
    dma = pltpu.SemaphoreType.DMA
    hbm = pl.BlockSpec(memory_space=pl.ANY)
    vmem = pl.BlockSpec(memory_space=pltpu.VMEM)
    best, cent = pl.pallas_call(
        kernel,
        out_shape=(
            jax.ShapeDtypeStruct((1, rows), F32),
            jax.ShapeDtypeStruct((clusters, width), F32),
        ),
        in_specs=[hbm, vmem, vmem, hbm, pl.BlockSpec(memory_space=pltpu.SMEM), hbm],
        out_specs=(vmem, vmem),
        scratch_shapes=[
            pltpu.VMEM((rows, width), BF16),
            pltpu.VMEM((clusters * depth, width), BF16),
            pltpu.VMEM((clusters * depth, 128), F32),
            pltpu.VMEM((clusters * depth, 128), F32),
            pltpu.VMEM((1, rows), jnp.int32),
            pltpu.VMEM((64, 16, width), BF16),
            pltpu.VMEM((64, 16, width), BF16),
            pltpu.VMEM((8, 1, 128), F32),
            pltpu.VMEM((64, 1, 128), F32),
            pltpu.VMEM((8, 1, 128), F32),
            pltpu.VMEM((64, 1, 128), F32),
            pltpu.VMEM((8, 128), F32),
            pltpu.VMEM((clusters, width), F32),
            pltpu.VMEM((clusters // 4, width), F32),
            pltpu.VMEM((3, clusters // 4, width), F32),
            pltpu.VMEM((3, clusters // 4, width), F32),
            pltpu.VMEM((4, clusters // 4, width), F32),
            dma((2,)), dma, dma,
            dma((8,)), dma((8,)), dma((8,)), dma((8,)), dma((8,)), dma((8,)),
            dma((3,)), dma((3,)), dma((3,)), dma((3,)),
        ],
        compiler_params=pltpu.CompilerParams(
            collective_id=0, has_side_effects=True, vmem_limit_bytes=56 << 20
        ),
        name="semdedup_round",
    )(
        arrivals,
        home_owner.reshape(1, rows),
        cluster_slot.reshape(1, rows),
        bank.reshape(clusters * depth, width),
        members,
        centroid_sum,
    )
    return best.reshape(rows), cent


def solution(mesh):
    return jax.shard_map(
        body,
        mesh=mesh,
        in_specs=(
            P(("grp", "own"), None),
            P(("grp", "own"), None),
            P(("grp", "own")),
            P("own", None, None),
            P("own"),
            P("own", None),
        ),
        out_specs=(P(("grp", "own")), P("own", None)),
        check_vma=False,
    )
```

time: 121 us -> 64.5 us (0.53)
  the two profiles are of different devices: /device:TPU:8 before, /device:TPU:1 now
where the time goes in v1:
time: 64.5 us; the launch traced here: 64.4 us
  Pallas kernels  60.6 us (94%)
  local copies, waits for them, and re-layouts  3.12 us (5%)
    pallas_call x1, Pallas kernels, body(): pl.pallas_call(kernel, out_shape=(jax.ShapeDtypeStruct((1, rows), F32), j...  60.6 us
    unnamed x2, local copies, waits for them, and re-layouts  3.12 us

profile of v1, /device:TPU:1, one launch (start us, length us, event | category | flops | bytes accessed | tf_op | source)
XLA Modules:
  0.0 64.4 jit_solution(7813192534707517536)
XLA Ops:
  0.6 60.6 %semdedup_round.1 = (f32[1,512]{1,0:T(1,128)}, f32[256,512]{1,0:T(8,128)}) custom-call(bf16[512,512]{1,0:T(8,128)(2,1)} %arr_h.1, s32[1,512]{1,0:T(1,128)} %bitcast.5, s32[1,512]{1,0:T(1,128)} %bitcast.6, bf16[8192,512]{1,0:T(8,128)(2,1)} %bitcast.4, s32[256]{0:T(256)} %mem.1, f32[256,512]{1,0:T(8,128)} %csum_h.1), custom_call_target="tpu_custom_call" | custom-call | tf_op jit(solution)/shard_map/semdedup_round/pallas_call | solution.py:273
  61.2 1.3 %copy.10 = f32[512]{0:T(512)} copy(f32[512]{0:T(512)} %bitcast.7) | data formatting | bytes 4096
  62.5 1.9 %copy.11 = f32[256,512]{1,0:T(8,128)} copy(f32[256,512]{1,0:T(8,128)} %get-tuple-element.9) | data formatting | bytes 1048576

commit v2 on v1

--- a/solution.py
+++ b/solution.py
@@ -9,10 +9,10 @@
 
 EPS = 1e-06
 MESH = pl.DeviceIdType.MESH
-Z_ORDER = (4, 0, 3, 5, 2, 6, 1, 7)
-SELF_GROUP = Z_ORDER.index(0)
+Z_ORDER = (3, 5, 4, 0, 2, 6, 1, 7)
+SELF_GROUP, HALF_RING = Z_ORDER.index(0), Z_ORDER.index(4)
 F32, BF16 = jnp.float32, jnp.bfloat16
-TILE = 512
+TILE = 2048
 
 
 def nt(a, b):
@@ -30,9 +30,9 @@
 def kernel(
     arr_h, tgt, slot, bank_h, mem, csum_h, best_o, cent_o,
     arr, bank, rn, colc, kbuf, send, recv, scode, rcode, bests, ret, r8,
-    acc, csum, rs_out, rs_in, ag,
+    acc, csum, relay, passed, onward, partial, ag,
     in_sem, bank_sem, self_sem, row_ss, row_rs, code_ss, code_rs, ret_ss, ret_rs,
-    rs_ss, rs_rs, ag_ss, ag_rs,
+    relay_sem, rs_ss, rs_rs, ag_ss, ag_rs,
 ):
     g = lax.axis_index("grp")
     me = lax.axis_index("own")
@@ -86,13 +86,13 @@
     unit = (
         values / jnp.sqrt(jnp.sum(values * values, axis=1, keepdims=True) + EPS)
     ).astype(BF16)
-    iota128 = lax.broadcasted_iota(jnp.int32, (128, rows), 0)
+    match = (lax.broadcasted_iota(jnp.int32, (1024, rows), 0) == k).astype(F32).astype(BF16)
+    send[...] = (
+        jnp.dot(match, unit, preferred_element_type=F32).astype(BF16).reshape(64, 16, -1)
+    )
+    sent_codes = nt(code_row, match)[0:1, :] - 1.0
     for zi in range(8):
-        match = (iota128 + zi * 128 == k).astype(F32).astype(BF16)
-        send[pl.ds(zi * 8, 8)] = (
-            jnp.dot(match, unit, preferred_element_type=F32).astype(BF16).reshape(8, 16, -1)
-        )
-        scode[zi] = nt(code_row, match)[0:1, :] - 1.0
+        scode[zi] = sent_codes[:, zi * 128 : zi * 128 + 128]
 
     pl.semaphore_wait(barrier, 66)
 
@@ -121,26 +121,57 @@
         return pltpu.make_async_remote_copy(
             src_ref=buf.at[part], dst_ref=buf.at[part], send_sem=sem.at[zi],
             recv_sem=sem.at[zi], device_id=(g, me), device_id_type=MESH,
+        )
+
+    def piece(far, half):
+        start = lax.rem(g + far, 4) * quarter + half * (quarter // 2)
+        return pl.ds(pl.multiple_of(start, quarter // 2), quarter // 2)
+
+    def to_next(src, dst, ss, rs, step, side):
+        return pltpu.make_async_remote_copy(
+            src_ref=src, dst_ref=dst, send_sem=ss.at[step * 2 + side],
+            recv_sem=rs.at[step * 2 + side],
+            device_id=(lax.rem(g + (1 if side == 0 else 3), 4), me), device_id_type=MESH,
         )
 
     me_slot = SELF_GROUP * 8
     self_cp = pltpu.make_async_copy(send.at[me_slot], recv.at[me_slot], self_sem)
     self_cp.start()
     rcode[me_slot] = scode[SELF_GROUP]
-    for chunk in range(4):
-        @pl.loop(0, 8)
-        def _(q):
-            for zi in (2 * chunk, 2 * chunk + 1):
-                if zi != SELF_GROUP:
-                    dev = peer(x, z, c, Z_ORDER[zi], q, 1)
-                    code_copy(zi, q, dev).start()
-                    row_copy(zi, q, 1, dev).start()
-        if SELF_GROUP // 2 == chunk:
-            @pl.loop(1, 8)
-            def _(q):
-                dev = peer(x, z, c, 0, q, 1)
-                code_copy(SELF_GROUP, q, dev).start()
-                row_copy(SELF_GROUP, q, 1, dev).start()
+
+    def send_rows(zi, q):
+        dev = peer(x, z, c, Z_ORDER[zi], q, 1)
+        code_copy(zi, q, dev).start()
+        row_copy(zi, q, 1, dev).start()
+
+    def first_leg(q, dev):
+        return pltpu.make_async_remote_copy(
+            src_ref=send.at[HALF_RING * 8 + q], dst_ref=relay.at[q - 4],
+            send_sem=row_ss.at[HALF_RING], recv_sem=relay_sem.at[0],
+            device_id=(g, dev), device_id_type=MESH,
+        )
+
+    def second_leg(dev):
+        return pltpu.make_async_remote_copy(
+            src_ref=relay, dst_ref=recv.at[pl.ds(HALF_RING * 8 + 4, 4)],
+            send_sem=relay_sem.at[1], recv_sem=row_rs.at[HALF_RING],
+            device_id=(g, dev), device_id_type=MESH,
+        )
+
+    @pl.loop(0, 4)
+    def _(q):
+        send_rows(HALF_RING, q)
+        code_copy(HALF_RING, q + 4, peer(x, z, c, 4, q + 4, 1)).start()
+        first_leg(q + 4, peer(x, z, c, 6, q + 4, 1)).start()
+
+    @pl.loop(1, 8)
+    def _(q):
+        send_rows(SELF_GROUP, q)
+
+    @pl.loop(0, 8)
+    def _(q):
+        send_rows(0, q)
+        send_rows(1, q)
 
     @pl.loop(0, clusters)
     def _(cl):
@@ -157,6 +188,22 @@
         b = bank[part, :].astype(F32)
         norm = 1.0 / jnp.sqrt(jnp.sum(b * b, axis=1, keepdims=True) + EPS)
         rn[part, :] = jnp.broadcast_to(norm, (256, 128))
+
+    pltpu.make_async_remote_copy(
+        src_ref=relay, dst_ref=relay, send_sem=relay_sem.at[0], recv_sem=relay_sem.at[0],
+        device_id=(g, me), device_id_type=MESH,
+    ).wait_recv()
+    second_leg(peer(x, z, c, 6, 0, 1)).start()
+
+    @pl.loop(0, 8)
+    def _(q):
+        send_rows(4, q)
+        send_rows(5, q)
+
+    @pl.loop(0, 8)
+    def _(q):
+        send_rows(6, q)
+        send_rows(7, q)
 
     lane16 = lax.broadcasted_iota(jnp.int32, (1, 128), 1) // 16
 
@@ -185,10 +232,13 @@
         ).astype(F32).astype(BF16)
         acc[...] += jnp.dot(which, q_rows, preferred_element_type=F32)
         if chunk == 3:
-            for j in range(1, 4):
-                to = lax.rem(g + j, 4)
-                rs_out[j - 1] = acc[pl.ds(to * quarter, quarter), :]
-                rs_copy(g, me, j, rs_out, rs_in, rs_ss, rs_rs).start()
+            for side in range(2):
+                to_next(acc.at[piece(2, side)], passed.at[side], rs_ss, rs_rs, 0, side).start()
+            for side in range(2):
+                to_next(
+                    acc.at[piece(1 if side == 0 else 3, 1 - side)], partial.at[side, 1 - side],
+                    rs_ss, rs_rs, 1, side,
+                ).start()
 
         def tile(i, best):
             part = pl.ds(pl.multiple_of(i * TILE, TILE), TILE)
@@ -214,14 +264,28 @@
             def _(q):
                 ret_copy(zi, q, peer(x, z, c, Z_ORDER[zi], q, -1)).start()
 
+    for side in range(2):
+        to_next(passed.at[side], passed.at[side], rs_ss, rs_rs, 0, side).wait_recv()
+        onward[side] = passed[side] + acc[piece(1 if side == 0 else 3, side)]
+        to_next(onward.at[side], partial.at[side, side], rs_ss, rs_rs, 2, side).start()
     csum_cp.wait()
-    total = csum[...] + acc[pl.ds(g * quarter, quarter), :]
-    for j in range(1, 4):
-        rs_copy(g, me, j, rs_out, rs_in, rs_ss, rs_rs).wait_recv()
-        total += rs_in[j - 1]
-    ag[g] = total / jnp.sqrt(jnp.sum(total * total, axis=1, keepdims=True) + EPS)
-    for j in range(1, 4):
-        ag_copy(g, me, j, ag, ag_ss, ag_rs, g).start()
+    mine = pl.ds(pl.multiple_of(g * quarter, quarter), quarter)
+    total = csum[...] + acc[mine, :]
+    for side in range(2):
+        for step, half in ((1, 1 - side), (2, side)):
+            landing = partial.at[side, half]
+            to_next(landing, landing, rs_ss, rs_rs, step, side).wait_recv()
+        total += partial[side].reshape(quarter, -1)
+    unit_total = total / jnp.sqrt(jnp.sum(total * total, axis=1, keepdims=True) + EPS)
+    ag[g] = unit_total.reshape(2, quarter // 2, -1)
+    for step in range(2):
+        for side in range(2):
+            half = ag.at[g, side if step == 0 else 1 - side]
+            to_next(half, half, ag_ss, ag_rs, step, side).start()
+    for side in range(2):
+        half = ag.at[lax.rem(g + 3 + 2 * side, 4), side]
+        to_next(half, half, ag_ss, ag_rs, 0, side).wait_recv()
+        to_next(half, half, ag_ss, ag_rs, 2, side).start()
 
     for zi in range(8):
         landed(ret, zi, ret_rs).wait_recv()
@@ -229,39 +293,31 @@
         r8[zi : zi + 1, :] = folded(ret, zi)
     k = kbuf[...]
     group = (lax.broadcasted_iota(jnp.int32, (8, rows), 0) == (k >> 7)).astype(F32)
+    lane_of = lax.broadcasted_iota(jnp.int32, (128, rows), 0)
     spread = lax.dot_general(
         r8[...], group, (((0,), (0,)), ((), ())),
         preferred_element_type=F32, precision=lax.Precision.HIGHEST,
     )
     best_o[...] = jnp.sum(
-        jnp.where(iota128 == (k & 127), spread, 0.0), axis=0, keepdims=True
-    )
-
-    for j in range(1, 4):
-        ag_copy(g, me, j, ag, ag_ss, ag_rs, lax.rem(g + 4 - j, 4)).wait_recv()
+        jnp.where(lane_of == (k & 127), spread, 0.0), axis=0, keepdims=True
+    )
+
+    for side in range(2):
+        for step, far, half in ((1, 3 + 2 * side, 1 - side), (2, 2, side)):
+            landing = ag.at[lax.rem(g + far, 4), half]
+            to_next(landing, landing, ag_ss, ag_rs, step, side).wait_recv()
     cent_o[...] = ag[...].reshape(clusters, -1)
 
     for zi in range(8):
         landed(send, zi, row_ss).wait_send()
         landed(rcode, zi, code_ss).wait_send()
         landed(ret, zi, ret_ss).wait_send()
-    for j in range(1, 4):
-        rs_copy(g, me, j, rs_out, rs_in, rs_ss, rs_rs).wait_send()
-        ag_copy(g, me, j, ag, ag_ss, ag_rs, g).wait_send()
-
-
-def rs_copy(g, me, j, rs_out, rs_in, ss, rs):
-    return pltpu.make_async_remote_copy(
-        src_ref=rs_out.at[j - 1], dst_ref=rs_in.at[j - 1], send_sem=ss.at[j - 1],
-        recv_sem=rs.at[j - 1], device_id=(lax.rem(g + j, 4), me), device_id_type=MESH,
-    )
-
-
-def ag_copy(g, me, j, ag, ss, rs, at):
-    return pltpu.make_async_remote_copy(
-        src_ref=ag.at[at], dst_ref=ag.at[at], send_sem=ss.at[j - 1],
-        recv_sem=rs.at[j - 1], device_id=(lax.rem(g + j, 4), me), device_id_type=MESH,
-    )
+    second_leg(me).wait_send()
+    for step in range(3):
+        for side in range(2):
+            half = passed.at[side]
+            to_next(half, half, rs_ss, rs_rs, step, side).wait_send()
+            to_next(half, half, ag_ss, ag_rs, step, side).wait_send()
 
 
 def body(arrivals, home_owner, cluster_slot, bank, members, centroid_sum):
@@ -293,12 +349,14 @@
             pltpu.VMEM((8, 128), F32),
             pltpu.VMEM((clusters, width), F32),
             pltpu.VMEM((clusters // 4, width), F32),
-            pltpu.VMEM((3, clusters // 4, width), F32),
-            pltpu.VMEM((3, clusters // 4, width), F32),
-            pltpu.VMEM((4, clusters // 4, width), F32),
+            pltpu.VMEM((4, 16, width), BF16),
+            pltpu.VMEM((2, clusters // 8, width), F32),
+            pltpu.VMEM((2, clusters // 8, width), F32),
+            pltpu.VMEM((2, 2, clusters // 8, width), F32),
+            pltpu.VMEM((4, 2, clusters // 8, width), F32),
             dma((2,)), dma, dma,
             dma((8,)), dma((8,)), dma((8,)), dma((8,)), dma((8,)), dma((8,)),
-            dma((3,)), dma((3,)), dma((3,)), dma((3,)),
+            dma((2,)), dma((6,)), dma((6,)), dma((6,)), dma((6,)),
         ],
         compiler_params=pltpu.CompilerParams(
             collective_id=0, has_side_effects=True, vmem_limit_bytes=56 << 20

time: 64.5 us -> 63.3 us (0.981)
  the two profiles are of different devices: /device:TPU:1 before, /device:TPU:8 now
where the time goes in v2:
time: 63.3 us; the launch traced here: 63.1 us
  Pallas kernels  59.4 us (94%)
  local copies, waits for them, and re-layouts  3.12 us (5%)
  between operations  0.64 us (1%)
    pallas_call x1, Pallas kernels, body(): pl.pallas_call(kernel, out_shape=(jax.ShapeDtypeStruct((1, rows), F32), j...  59.4 us
    unnamed x2, local copies, waits for them, and re-layouts  3.12 us

profile of v2, /device:TPU:8, one launch (start us, length us, event | category | flops | bytes accessed | tf_op | source)
XLA Modules:
  0.0 63.1 jit_solution(10982950001544358999)
XLA Ops:
  0.6 59.4 %semdedup_round.1 = (f32[1,512]{1,0:T(1,128)}, f32[256,512]{1,0:T(8,128)}) custom-call(bf16[512,512]{1,0:T(8,128)(2,1)} %arr_h.1, s32[1,512]{1,0:T(1,128)} %bitcast.5, s32[1,512]{1,0:T(1,128)} %bitcast.6, bf16[8192,512]{1,0:T(8,128)(2,1)} %bitcast.4, s32[256]{0:T(256)} %mem.1, f32[256,512]{1,0:T(8,128)} %csum_h.1), custom_call_target="tpu_custom_call" | custom-call | tf_op jit(solution)/shard_map/semdedup_round/pallas_call | solution.py:329
  60.0 1.3 %copy.10 = f32[512]{0:T(512)} copy(f32[512]{0:T(512)} %bitcast.7) | data formatting | bytes 4096
  61.3 1.9 %copy.11 = f32[256,512]{1,0:T(8,128)} copy(f32[256,512]{1,0:T(8,128)} %get-tuple-element.9) | data formatting | bytes 1048576

commit v3 on v2

--- a/solution.py
+++ b/solution.py
@@ -9,8 +9,9 @@
 
 EPS = 1e-06
 MESH = pl.DeviceIdType.MESH
-Z_ORDER = (3, 5, 4, 0, 2, 6, 1, 7)
-SELF_GROUP, HALF_RING = Z_ORDER.index(0), Z_ORDER.index(4)
+Z_ORDER = (4, 0, 3, 5, 2, 6, 1, 7)
+LINE = (4, 3, 5, 2, 6, 1, 7)
+SELF_GROUP = Z_ORDER.index(0)
 F32, BF16 = jnp.float32, jnp.bfloat16
 TILE = 2048
 
@@ -30,9 +31,9 @@
 def kernel(
     arr_h, tgt, slot, bank_h, mem, csum_h, best_o, cent_o,
     arr, bank, rn, colc, kbuf, send, recv, scode, rcode, bests, ret, r8,
-    acc, csum, relay, passed, onward, partial, ag,
+    acc, csum, passed, onward, partial, ag,
     in_sem, bank_sem, self_sem, row_ss, row_rs, code_ss, code_rs, ret_ss, ret_rs,
-    relay_sem, rs_ss, rs_rs, ag_ss, ag_rs,
+    rs_ss, rs_rs, ag_ss, ag_rs, met, out_sem,
 ):
     g = lax.axis_index("grp")
     me = lax.axis_index("own")
@@ -50,12 +51,15 @@
     bank_cp.start()
 
     barrier = pltpu.get_barrier_semaphore()
-    for zi, dz in enumerate(Z_ORDER):
-        @pl.loop(1 if zi == SELF_GROUP else 0, 8)
-        def _(q):
-            pl.semaphore_signal(
-                barrier, inc=1, device_id=(g, peer(x, z, c, dz, q, 1)), device_id_type=MESH
-            )
+    for dz in LINE:
+        pl.semaphore_signal(
+            barrier, inc=1, device_id=(g, peer(x, z, c, dz, 0, 1)), device_id_type=MESH
+        )
+    @pl.loop(1, 8)
+    def _(q):
+        pl.semaphore_signal(
+            barrier, inc=1, device_id=(g, peer(x, z, c, 0, q, 1)), device_id_type=MESH
+        )
     for j in range(1, 4):
         pl.semaphore_signal(
             barrier, inc=1, device_id=(lax.rem(g + j, 4), me), device_id_type=MESH
@@ -94,7 +98,12 @@
     for zi in range(8):
         scode[zi] = sent_codes[:, zi * 128 : zi * 128 + 128]
 
-    pl.semaphore_wait(barrier, 66)
+    pl.semaphore_wait(barrier, 17)
+    @pl.loop(1, 8)
+    def _(q):
+        pl.semaphore_signal(
+            met, inc=1, device_id=(g, peer(x, z, c, 0, q, 1)), device_id_type=MESH
+        )
 
     def row_copy(zi, lo, n, dev):
         part = pl.ds(zi * 8 + lo, n)
@@ -144,34 +153,20 @@
         code_copy(zi, q, dev).start()
         row_copy(zi, q, 1, dev).start()
 
-    def first_leg(q, dev):
-        return pltpu.make_async_remote_copy(
-            src_ref=send.at[HALF_RING * 8 + q], dst_ref=relay.at[q - 4],
-            send_sem=row_ss.at[HALF_RING], recv_sem=relay_sem.at[0],
-            device_id=(g, dev), device_id_type=MESH,
-        )
-
-    def second_leg(dev):
-        return pltpu.make_async_remote_copy(
-            src_ref=relay, dst_ref=recv.at[pl.ds(HALF_RING * 8 + 4, 4)],
-            send_sem=relay_sem.at[1], recv_sem=row_rs.at[HALF_RING],
-            device_id=(g, dev), device_id_type=MESH,
-        )
-
-    @pl.loop(0, 4)
-    def _(q):
-        send_rows(HALF_RING, q)
-        code_copy(HALF_RING, q + 4, peer(x, z, c, 4, q + 4, 1)).start()
-        first_leg(q + 4, peer(x, z, c, 6, q + 4, 1)).start()
+    for dz in LINE:
+        send_rows(Z_ORDER.index(dz), 0)
 
     @pl.loop(1, 8)
     def _(q):
         send_rows(SELF_GROUP, q)
 
-    @pl.loop(0, 8)
-    def _(q):
-        send_rows(0, q)
-        send_rows(1, q)
+    pl.semaphore_wait(met, 7)
+
+    for pair in ((4,), (3, 5), (2, 6), (1, 7)):
+        @pl.loop(1, 8)
+        def _(q):
+            for dz in pair:
+                send_rows(Z_ORDER.index(dz), q)
 
     @pl.loop(0, clusters)
     def _(cl):
@@ -188,22 +183,6 @@
         b = bank[part, :].astype(F32)
         norm = 1.0 / jnp.sqrt(jnp.sum(b * b, axis=1, keepdims=True) + EPS)
         rn[part, :] = jnp.broadcast_to(norm, (256, 128))
-
-    pltpu.make_async_remote_copy(
-        src_ref=relay, dst_ref=relay, send_sem=relay_sem.at[0], recv_sem=relay_sem.at[0],
-        device_id=(g, me), device_id_type=MESH,
-    ).wait_recv()
-    second_leg(peer(x, z, c, 6, 0, 1)).start()
-
-    @pl.loop(0, 8)
-    def _(q):
-        send_rows(4, q)
-        send_rows(5, q)
-
-    @pl.loop(0, 8)
-    def _(q):
-        send_rows(6, q)
-        send_rows(7, q)
 
     lane16 = lax.broadcasted_iota(jnp.int32, (1, 128), 1) // 16
 
@@ -234,11 +213,6 @@
         if chunk == 3:
             for side in range(2):
                 to_next(acc.at[piece(2, side)], passed.at[side], rs_ss, rs_rs, 0, side).start()
-            for side in range(2):
-                to_next(
-                    acc.at[piece(1 if side == 0 else 3, 1 - side)], partial.at[side, 1 - side],
-                    rs_ss, rs_rs, 1, side,
-                ).start()
 
         def tile(i, best):
             part = pl.ds(pl.multiple_of(i * TILE, TILE), TILE)
@@ -253,7 +227,22 @@
             return tuple(new)
 
         start = jnp.full((8, 128), -3.0, F32)
-        best = lax.fori_loop(0, bank.shape[0] // TILE, tile, (start, start))
+        tiles = bank.shape[0] // TILE
+        if chunk < 3:
+            best = lax.fori_loop(0, tiles, tile, (start, start))
+        else:
+            best = tile(0, (start, start))
+            for side in range(2):
+                to_next(
+                    acc.at[piece(1 if side == 0 else 3, 1 - side)], partial.at[side, 1 - side],
+                    rs_ss, rs_rs, 1, side,
+                ).start()
+            best = lax.fori_loop(1, tiles - 1, tile, best)
+            for side in range(2):
+                to_next(passed.at[side], passed.at[side], rs_ss, rs_rs, 0, side).wait_recv()
+                onward[side] = passed[side] + acc[piece(1 if side == 0 else 3, side)]
+                to_next(onward.at[side], partial.at[side, side], rs_ss, rs_rs, 2, side).start()
+            best = tile(tiles - 1, best)
         for h in range(2):
             zi = 2 * chunk + h
             bests[zi] = jnp.max(best[h], axis=0, keepdims=True)
@@ -264,10 +253,6 @@
             def _(q):
                 ret_copy(zi, q, peer(x, z, c, Z_ORDER[zi], q, -1)).start()
 
-    for side in range(2):
-        to_next(passed.at[side], passed.at[side], rs_ss, rs_rs, 0, side).wait_recv()
-        onward[side] = passed[side] + acc[piece(1 if side == 0 else 3, side)]
-        to_next(onward.at[side], partial.at[side, side], rs_ss, rs_rs, 2, side).start()
     csum_cp.wait()
     mine = pl.ds(pl.multiple_of(g * quarter, quarter), quarter)
     total = csum[...] + acc[mine, :]
@@ -278,14 +263,31 @@
         total += partial[side].reshape(quarter, -1)
     unit_total = total / jnp.sqrt(jnp.sum(total * total, axis=1, keepdims=True) + EPS)
     ag[g] = unit_total.reshape(2, quarter // 2, -1)
-    for step in range(2):
+
+    def publish(far, half):
+        at = lax.rem(g + far, 4)
+        return pltpu.make_async_copy(
+            ag.at[at, half], cent_o.at[at, half], out_sem.at[far * 2 + half]
+        )
+
+    def spread_mine(step):
         for side in range(2):
             half = ag.at[g, side if step == 0 else 1 - side]
             to_next(half, half, ag_ss, ag_rs, step, side).start()
+            if step == 0:
+                publish(0, side).start()
+
+    spread_mine(0)
+
+    for side in range(2):
+        half = ag.at[g, side]
+        to_next(half, half, ag_ss, ag_rs, 0, side).wait_send()
+    spread_mine(1)
     for side in range(2):
         half = ag.at[lax.rem(g + 3 + 2 * side, 4), side]
         to_next(half, half, ag_ss, ag_rs, 0, side).wait_recv()
         to_next(half, half, ag_ss, ag_rs, 2, side).start()
+        publish(3 if side == 0 else 1, side).start()
 
     for zi in range(8):
         landed(ret, zi, ret_rs).wait_recv()
@@ -303,21 +305,24 @@
     )
 
     for side in range(2):
-        for step, far, half in ((1, 3 + 2 * side, 1 - side), (2, 2, side)):
+        for step, far, half in ((1, 3 - 2 * side, 1 - side), (2, 2, side)):
             landing = ag.at[lax.rem(g + far, 4), half]
             to_next(landing, landing, ag_ss, ag_rs, step, side).wait_recv()
-    cent_o[...] = ag[...].reshape(clusters, -1)
+            publish(far, half).start()
+    for far in range(4):
+        for half in range(2):
+            publish(far, half).wait()
 
     for zi in range(8):
         landed(send, zi, row_ss).wait_send()
         landed(rcode, zi, code_ss).wait_send()
         landed(ret, zi, ret_ss).wait_send()
-    second_leg(me).wait_send()
     for step in range(3):
         for side in range(2):
             half = passed.at[side]
             to_next(half, half, rs_ss, rs_rs, step, side).wait_send()
-            to_next(half, half, ag_ss, ag_rs, step, side).wait_send()
+            if step > 0:
+                to_next(half, half, ag_ss, ag_rs, step, side).wait_send()
 
 
 def body(arrivals, home_owner, cluster_slot, bank, members, centroid_sum):
@@ -330,10 +335,10 @@
         kernel,
         out_shape=(
             jax.ShapeDtypeStruct((1, rows), F32),
-            jax.ShapeDtypeStruct((clusters, width), F32),
+            jax.ShapeDtypeStruct((4, 2, clusters // 8, width), F32),
         ),
         in_specs=[hbm, vmem, vmem, hbm, pl.BlockSpec(memory_space=pltpu.SMEM), hbm],
-        out_specs=(vmem, vmem),
+        out_specs=(vmem, hbm),
         scratch_shapes=[
             pltpu.VMEM((rows, width), BF16),
             pltpu.VMEM((clusters * depth, width), BF16),
@@ -349,14 +354,14 @@
             pltpu.VMEM((8, 128), F32),
             pltpu.VMEM((clusters, width), F32),
             pltpu.VMEM((clusters // 4, width), F32),
-            pltpu.VMEM((4, 16, width), BF16),
             pltpu.VMEM((2, clusters // 8, width), F32),
             pltpu.VMEM((2, clusters // 8, width), F32),
             pltpu.VMEM((2, 2, clusters // 8, width), F32),
             pltpu.VMEM((4, 2, clusters // 8, width), F32),
             dma((2,)), dma, dma,
             dma((8,)), dma((8,)), dma((8,)), dma((8,)), dma((8,)), dma((8,)),
-            dma((2,)), dma((6,)), dma((6,)), dma((6,)), dma((6,)),
+            dma((6,)), dma((6,)), dma((6,)), dma((6,)),
+            pltpu.SemaphoreType.REGULAR, dma((8,)),
         ],
         compiler_params=pltpu.CompilerParams(
             collective_id=0, has_side_effects=True, vmem_limit_bytes=56 << 20
@@ -370,7 +375,7 @@
         members,
         centroid_sum,
     )
-    return best.reshape(rows), cent
+    return best.reshape(rows), cent.reshape(clusters, width)
 
 
 def solution(mesh):

time: 63.3 us -> 59.1 us (0.934)
  Pallas kernels: 59.4 us -> 55.2 us
    pallas_call x1, Pallas kernels: 59.4 us -> 55.2 us  [body(): pl.pallas_call(kernel, out_shape=(jax.ShapeDtypeStruct((1, rows), F32), j...]
where the time goes in v3:
time: 59.1 us; the launch traced here: 58.9 us
  Pallas kernels  55.2 us (93%)
  local copies, waits for them, and re-layouts  3.12 us (5%)
  between operations  0.64 us (1%)
    pallas_call x1, Pallas kernels, body(): pl.pallas_call(kernel, out_shape=(jax.ShapeDtypeStruct((1, rows), F32), j...  55.2 us
    unnamed x2, local copies, waits for them, and re-layouts  3.12 us

profile of v3, /device:TPU:8, one launch (start us, length us, event | category | flops | bytes accessed | tf_op | source)
XLA Modules:
  0.0 58.9 jit_solution(13732176240389529227)
XLA Ops:
  0.6 55.2 %semdedup_round.1 = (f32[1,512]{1,0:T(1,128)}, f32[4,2,32,512]{3,2,1,0:T(8,128)}) custom-call(bf16[512,512]{1,0:T(8,128)(2,1)} %arr_h.1, s32[1,512]{1,0:T(1,128)} %bitcast.7, s32[1,512]{1,0:T(1,128)} %bitcast.8, bf16[8192,512]{1,0:T(8,128)(2,1)} %bitcast.5, s32[256]{0:T(256)} %mem.1, f32[256,512]{1,0:T(8,128)} %csum_h.1), custom_call_target="tpu_custom_call" | custom-call | tf_op jit(solution)/shard_map/semdedup_round/pallas_call | solution.py:334
  55.8 1.3 %copy.10 = f32[512]{0:T(512)} copy(f32[512]{0:T(512)} %bitcast.9) | data formatting | bytes 4096
  57.1 1.9 %copy.11 = f32[256,512]{1,0:T(8,128)} copy(f32[256,512]{1,0:T(8,128)} %bitcast.6) | data formatting | bytes 1048576

commit v4 on v3

--- a/solution.py
+++ b/solution.py
@@ -29,8 +29,8 @@
 
 
 def kernel(
-    arr_h, tgt, slot, bank_h, mem, csum_h, best_o, cent_o,
-    arr, bank, rn, colc, kbuf, send, recv, scode, rcode, bests, ret, r8,
+    arr_h, tgt_h, slot_h, bank_h, mem_h, csum_h, best_o, cent_o,
+    tgt, slot, mem, arr, bank, rn, colc, kbuf, send, recv, scode, zcode, rcode, bests, ret, r8,
     acc, csum, passed, onward, partial, ag,
     in_sem, bank_sem, self_sem, row_ss, row_rs, code_ss, code_rs, ret_ss, ret_rs,
     rs_ss, rs_rs, ag_ss, ag_rs, met, out_sem,
@@ -38,9 +38,28 @@
     g = lax.axis_index("grp")
     me = lax.axis_index("own")
     x, z, c = me // 16, lax.rem(me // 2, 8), lax.rem(me, 2)
-    clusters = mem.shape[0]
+    clusters = mem_h.shape[0]
     quarter = clusters // 4
 
+    barrier = pltpu.get_barrier_semaphore()
+    for dz in LINE:
+        pl.semaphore_signal(
+            barrier, inc=1, device_id=(g, peer(x, z, c, dz, 0, 1)), device_id_type=MESH
+        )
+    @pl.loop(1, 8)
+    def _(q):
+        pl.semaphore_signal(
+            barrier, inc=1, device_id=(g, peer(x, z, c, 0, q, 1)), device_id_type=MESH
+        )
+    for j in range(1, 4):
+        pl.semaphore_signal(
+            barrier, inc=1, device_id=(lax.rem(g + j, 4), me), device_id_type=MESH
+        )
+
+    tgt_cp = pltpu.make_async_copy(tgt_h, tgt, in_sem.at[2])
+    tgt_cp.start()
+    slot_cp = pltpu.make_async_copy(slot_h, slot, in_sem.at[3])
+    slot_cp.start()
     arr_cp = pltpu.make_async_copy(arr_h, arr, in_sem.at[0])
     arr_cp.start()
     csum_cp = pltpu.make_async_copy(
@@ -49,22 +68,10 @@
     csum_cp.start()
     bank_cp = pltpu.make_async_copy(bank_h, bank, bank_sem)
     bank_cp.start()
-
-    barrier = pltpu.get_barrier_semaphore()
-    for dz in LINE:
-        pl.semaphore_signal(
-            barrier, inc=1, device_id=(g, peer(x, z, c, dz, 0, 1)), device_id_type=MESH
-        )
-    @pl.loop(1, 8)
-    def _(q):
-        pl.semaphore_signal(
-            barrier, inc=1, device_id=(g, peer(x, z, c, 0, q, 1)), device_id_type=MESH
-        )
-    for j in range(1, 4):
-        pl.semaphore_signal(
-            barrier, inc=1, device_id=(lax.rem(g + j, 4), me), device_id_type=MESH
-        )
-
+    mem_cp = pltpu.make_async_copy(mem_h, mem, in_sem.at[4])
+    mem_cp.start()
+
+    tgt_cp.wait()
     t = tgt[...]
     dx = ((t >> 4) - x) & 3
     dz = ((t >> 1) - z) & 7
@@ -83,6 +90,7 @@
     placed = jnp.sum(jnp.where(hit, earlier, 0.0), axis=0, keepdims=True).astype(jnp.int32)
     k = pos * 16 + placed
     kbuf[...] = k
+    slot_cp.wait()
     code_row = jnp.broadcast_to((slot[...] + 1).astype(F32), (8, rows)).astype(BF16)
 
     arr_cp.wait()
@@ -112,10 +120,24 @@
             recv_sem=row_rs.at[zi], device_id=(g, dev), device_id_type=MESH,
         )
 
-    def code_copy(zi, q, dev):
-        return pltpu.make_async_remote_copy(
-            src_ref=scode.at[zi], dst_ref=rcode.at[zi * 8 + q], send_sem=code_ss.at[zi],
-            recv_sem=code_rs.at[zi], device_id=(g, dev), device_id_type=MESH,
+    def code_z(zi):
+        return pltpu.make_async_remote_copy(
+            src_ref=scode.at[zi], dst_ref=zcode.at[zi], send_sem=code_ss.at[zi],
+            recv_sem=code_rs.at[zi], device_id=(g, peer(x, z, c, Z_ORDER[zi], 0, 1)),
+            device_id_type=MESH,
+        )
+
+    def code_x(q, dev):
+        return pltpu.make_async_remote_copy(
+            src_ref=zcode, dst_ref=rcode.at[q], send_sem=code_ss.at[SELF_GROUP],
+            recv_sem=code_rs.at[SELF_GROUP], device_id=(g, dev), device_id_type=MESH,
+        )
+
+    def codes_x():
+        return pltpu.make_async_remote_copy(
+            src_ref=rcode.at[pl.ds(1, 7)], dst_ref=rcode.at[pl.ds(1, 7)],
+            send_sem=code_ss.at[SELF_GROUP], recv_sem=code_rs.at[SELF_GROUP],
+            device_id=(g, me), device_id_type=MESH,
         )
 
     def ret_copy(zi, q, dev):
@@ -146,14 +168,14 @@
     me_slot = SELF_GROUP * 8
     self_cp = pltpu.make_async_copy(send.at[me_slot], recv.at[me_slot], self_sem)
     self_cp.start()
-    rcode[me_slot] = scode[SELF_GROUP]
+    zcode[SELF_GROUP] = scode[SELF_GROUP]
 
     def send_rows(zi, q):
         dev = peer(x, z, c, Z_ORDER[zi], q, 1)
-        code_copy(zi, q, dev).start()
         row_copy(zi, q, 1, dev).start()
 
     for dz in LINE:
+        code_z(Z_ORDER.index(dz)).start()
         send_rows(Z_ORDER.index(dz), 0)
 
     @pl.loop(1, 8)
@@ -168,6 +190,7 @@
             for dz in pair:
                 send_rows(Z_ORDER.index(dz), q)
 
+    mem_cp.wait()
     @pl.loop(0, clusters)
     def _(cl):
         live = lax.broadcasted_iota(jnp.int32, (32, 128), 0) < mem[cl]
@@ -184,12 +207,20 @@
         norm = 1.0 / jnp.sqrt(jnp.sum(b * b, axis=1, keepdims=True) + EPS)
         rn[part, :] = jnp.broadcast_to(norm, (256, 128))
 
+    for dz in LINE:
+        code_z(Z_ORDER.index(dz)).wait_recv()
+    rcode[0] = zcode[...]
+
+    @pl.loop(1, 8)
+    def _(q):
+        code_x(q, peer(x, z, c, 0, q, 1)).start()
+
     lane16 = lax.broadcasted_iota(jnp.int32, (1, 128), 1) // 16
 
-    def folded(buf, zi):
+    def folded(parts):
         total = jnp.zeros((1, 128), F32)
         for q in range(8):
-            total = jnp.where(lane16 == q, buf[zi * 8 + q], total)
+            total = jnp.where(lane16 == q, parts[q], total)
         return total
 
     def self_lo(zi):
@@ -200,10 +231,13 @@
         for zi in (2 * chunk, 2 * chunk + 1):
             lo = self_lo(zi)
             landed(recv, zi, row_rs).wait_recv()
-            landed(rcode, zi, code_rs).wait_recv()
             if lo:
                 self_cp.wait()
-        codes = [folded(rcode, zi) for zi in (2 * chunk, 2 * chunk + 1)]
+        if chunk == 0:
+            codes_x().wait_recv()
+        codes = [
+            folded([rcode[q, zi] for q in range(8)]) for zi in (2 * chunk, 2 * chunk + 1)
+        ]
         q_rows = recv[pl.ds(chunk * 16, 16)].reshape(256, -1)
         row_of = jnp.concatenate(codes, axis=1)
         which = (
@@ -249,9 +283,10 @@
             if zi == SELF_GROUP:
                 ret[me_slot] = bests[zi]
 
-            @pl.loop(self_lo(zi), 8)
-            def _(q):
-                ret_copy(zi, q, peer(x, z, c, Z_ORDER[zi], q, -1)).start()
+    for zi in range(8):
+        @pl.loop(self_lo(zi), 8)
+        def _(q):
+            ret_copy(zi, q, peer(x, z, c, Z_ORDER[zi], q, -1)).start()
 
     csum_cp.wait()
     mine = pl.ds(pl.multiple_of(g * quarter, quarter), quarter)
@@ -292,7 +327,7 @@
     for zi in range(8):
         landed(ret, zi, ret_rs).wait_recv()
     for zi in range(8):
-        r8[zi : zi + 1, :] = folded(ret, zi)
+        r8[zi : zi + 1, :] = folded([ret[zi * 8 + q] for q in range(8)])
     k = kbuf[...]
     group = (lax.broadcasted_iota(jnp.int32, (8, rows), 0) == (k >> 7)).astype(F32)
     lane_of = lax.broadcasted_iota(jnp.int32, (128, rows), 0)
@@ -315,14 +350,34 @@
 
     for zi in range(8):
         landed(send, zi, row_ss).wait_send()
-        landed(rcode, zi, code_ss).wait_send()
         landed(ret, zi, ret_ss).wait_send()
+    for dz in LINE:
+        code_z(Z_ORDER.index(dz)).wait_send()
+    codes_x().wait_send()
     for step in range(3):
         for side in range(2):
             half = passed.at[side]
             to_next(half, half, rs_ss, rs_rs, step, side).wait_send()
             if step > 0:
                 to_next(half, half, ag_ss, ag_rs, step, side).wait_send()
+
+
+def hand_on(best_i, cent_i, best_o, cent_o, best_v, cent_v, sem):
+    first = [
+        pltpu.make_async_copy(best_i, best_v, sem.at[0]),
+        pltpu.make_async_copy(cent_i, cent_v, sem.at[1]),
+    ]
+    for copy in first:
+        copy.start()
+    second = [
+        pltpu.make_async_copy(best_v, best_o, sem.at[2]),
+        pltpu.make_async_copy(cent_v, cent_o, sem.at[3]),
+    ]
+    for before, after in zip(first, second):
+        before.wait()
+        after.start()
+    for copy in second:
+        copy.wait()
 
 
 def body(arrivals, home_owner, cluster_slot, bank, members, centroid_sum):
@@ -337,9 +392,12 @@
             jax.ShapeDtypeStruct((1, rows), F32),
             jax.ShapeDtypeStruct((4, 2, clusters // 8, width), F32),
         ),
-        in_specs=[hbm, vmem, vmem, hbm, pl.BlockSpec(memory_space=pltpu.SMEM), hbm],
+        in_specs=[hbm] * 6,
         out_specs=(vmem, hbm),
         scratch_shapes=[
+            pltpu.VMEM((1, rows), jnp.int32),
+            pltpu.VMEM((1, rows), jnp.int32),
+            pltpu.SMEM((clusters,), jnp.int32),
             pltpu.VMEM((rows, width), BF16),
             pltpu.VMEM((clusters * depth, width), BF16),
             pltpu.VMEM((clusters * depth, 128), F32),
@@ -348,7 +406,8 @@
             pltpu.VMEM((64, 16, width), BF16),
             pltpu.VMEM((64, 16, width), BF16),
             pltpu.VMEM((8, 1, 128), F32),
-            pltpu.VMEM((64, 1, 128), F32),
+            pltpu.VMEM((8, 1, 128), F32),
+            pltpu.VMEM((8, 8, 1, 128), F32),
             pltpu.VMEM((8, 1, 128), F32),
             pltpu.VMEM((64, 1, 128), F32),
             pltpu.VMEM((8, 128), F32),
@@ -358,7 +417,7 @@
             pltpu.VMEM((2, clusters // 8, width), F32),
             pltpu.VMEM((2, 2, clusters // 8, width), F32),
             pltpu.VMEM((4, 2, clusters // 8, width), F32),
-            dma((2,)), dma, dma,
+            dma((5,)), dma, dma,
             dma((8,)), dma((8,)), dma((8,)), dma((8,)), dma((8,)), dma((8,)),
             dma((6,)), dma((6,)), dma((6,)), dma((6,)),
             pltpu.SemaphoreType.REGULAR, dma((8,)),
@@ -375,6 +434,16 @@
         members,
         centroid_sum,
     )
+    best, cent = pl.pallas_call(
+        hand_on,
+        out_shape=(
+            jax.ShapeDtypeStruct(best.shape, F32), jax.ShapeDtypeStruct(cent.shape, F32)
+        ),
+        in_specs=[hbm, hbm],
+        out_specs=(hbm, hbm),
+        scratch_shapes=[pltpu.VMEM(best.shape, F32), pltpu.VMEM(cent.shape, F32), dma((4,))],
+        name="hand_on",
+    )(best, cent)
     return best.reshape(rows), cent.reshape(clusters, width)
 
 

time: 59.1 us -> 56 us (0.948)
  local copies, waits for them, and re-layouts: 3.12 us -> 0 us
    unnamed x2 -> x0, local copies, waits for them, and re-layouts: 3.12 us -> none
    pallas_call x0 -> x1, Pallas kernels: none -> 1.87 us  [body(): pl.pallas_call(hand_on, out_shape=(jax.ShapeDtypeStruct(best.shape, F32),...]
    pallas_call x1, Pallas kernels: 55.2 us -> 53.3 us  [body(): pl.pallas_call(kernel, out_shape=(jax.ShapeDtypeStruct((1, rows), F32), j...]
where the time goes in v4:
time: 56 us; the launch traced here: 55.9 us
  Pallas kernels  55.2 us (99%)
  between operations  0.64 us (1%)
    pallas_call x1, Pallas kernels, body(): pl.pallas_call(kernel, out_shape=(jax.ShapeDtypeStruct((1, rows), F32), j...  53.3 us
    pallas_call x1, Pallas kernels, body(): pl.pallas_call(hand_on, out_shape=(jax.ShapeDtypeStruct(best.shape, F32),...  1.87 us

profile of v4, /device:TPU:8, one launch (start us, length us, event | category | flops | bytes accessed | tf_op | source)
XLA Modules:
  0.0 55.9 jit_solution(16337613995243441729)
XLA Ops:
  0.6 53.3 %semdedup_round.1 = (f32[1,512]{1,0:T(1,128)}, f32[4,2,32,512]{3,2,1,0:T(8,128)}) custom-call(bf16[512,512]{1,0:T(8,128)(2,1)} %arr_h.1, s32[1,512]{1,0:T(1,128)} %bitcast.6, s32[1,512]{1,0:T(1,128)} %bitcast.7, bf16[8192,512]{1,0:T(8,128)(2,1)} %bitcast.5, s32[256]{0:T(256)} %mem_h.1, f32[256,512]{1,0:T(8,128)} %csum_h.1), custom_call_target="tpu_custom_call" | custom-call | tf_op jit(solution)/shard_map/semdedup_round/pallas_call | solution.py:389
  54.0 1.9 %hand_on.1 = (f32[1,512]{1,0:T(1,128)}, f32[4,2,32,512]{3,2,1,0:T(8,128)}) custom-call(f32[1,512]{1,0:T(1,128)} %get-tuple-element.6.best_i, f32[4,2,32,512]{3,2,1,0:T(8,128)} %get-tuple-element.7.cent_i), custom_call_target="tpu_custom_call" | custom-call | tf_op jit(solution)/shard_map/hand_on/pallas_call | solution.py:437

commit v5 on v4

--- a/solution.py
+++ b/solution.py
@@ -14,6 +14,7 @@
 SELF_GROUP = Z_ORDER.index(0)
 F32, BF16 = jnp.float32, jnp.bfloat16
 TILE = 2048
+FACTOR, DEFER = 1, 1
 
 
 def nt(a, b):
@@ -226,6 +227,14 @@
     def self_lo(zi):
         return 1 if zi == SELF_GROUP else 0
 
+    def keep(chunk, best):
+        for h in range(2):
+            zi = 2 * chunk + h
+            bests[zi] = jnp.max(best[h], axis=0, keepdims=True)
+            if zi == SELF_GROUP:
+                ret[me_slot] = bests[zi]
+
+    deferred, held = [], None
     acc[...] = jnp.zeros_like(acc)
     for chunk in range(4):
         for zi in (2 * chunk, 2 * chunk + 1):
@@ -248,40 +257,50 @@
             for side in range(2):
                 to_next(acc.at[piece(2, side)], passed.at[side], rs_ss, rs_rs, 0, side).start()
 
-        def tile(i, best):
-            part = pl.ds(pl.multiple_of(i * TILE, TILE), TILE)
+        def tile(i, best, q_rows=q_rows, codes=codes, size=TILE):
+            part = pl.ds(pl.multiple_of(i * size, size), size)
             s = nt(bank[part, :], q_rows)
             scale, cols = rn[part, :], colc[part, :]
             new = []
             for h in range(2):
                 cand = jnp.where(
                     cols == codes[h], s[:, h * 128 : h * 128 + 128] * scale, -3.0
-                ).reshape(TILE // 8, 8, 128)
+                ).reshape(size // 8, 8, 128)
                 new.append(jnp.maximum(best[h], jnp.max(cand, axis=0)))
             return tuple(new)
 
         start = jnp.full((8, 128), -3.0, F32)
         tiles = bank.shape[0] // TILE
-        if chunk < 3:
-            best = lax.fori_loop(0, tiles, tile, (start, start))
+        if chunk < 2:
+            best = lax.fori_loop(
+                0, tiles // FACTOR, functools.partial(tile, size=FACTOR * TILE), (start, start)
+            )
+        elif chunk == 2:
+            best = lax.fori_loop(0, tiles - DEFER, tile, (start, start))
+            for n in range(DEFER):
+                deferred.append(functools.partial(tile, tiles - DEFER + n))
+            held = best
         else:
-            best = tile(0, (start, start))
+            for step in deferred:
+                held = step(held)
+            keep(2, held)
+            best = (start, start)
+            if not deferred:
+                best = tile(0, best)
             for side in range(2):
                 to_next(
                     acc.at[piece(1 if side == 0 else 3, 1 - side)], partial.at[side, 1 - side],
                     rs_ss, rs_rs, 1, side,
                 ).start()
-            best = lax.fori_loop(1, tiles - 1, tile, best)
+            done = tiles - 1 - DEFER
+            best = lax.fori_loop(0 if deferred else 1, done, tile, best)
             for side in range(2):
                 to_next(passed.at[side], passed.at[side], rs_ss, rs_rs, 0, side).wait_recv()
                 onward[side] = passed[side] + acc[piece(1 if side == 0 else 3, side)]
                 to_next(onward.at[side], partial.at[side, side], rs_ss, rs_rs, 2, side).start()
-            best = tile(tiles - 1, best)
-        for h in range(2):
-            zi = 2 * chunk + h
-            bests[zi] = jnp.max(best[h], axis=0, keepdims=True)
-            if zi == SELF_GROUP:
-                ret[me_slot] = bests[zi]
+            best = lax.fori_loop(done, tiles, tile, best)
+        if chunk != 2:
+            keep(chunk, best)
 
     for zi in range(8):
         @pl.loop(self_lo(zi), 8)
@@ -362,21 +381,14 @@
                 to_next(half, half, ag_ss, ag_rs, step, side).wait_send()
 
 
-def hand_on(best_i, cent_i, best_o, cent_o, best_v, cent_v, sem):
-    first = [
-        pltpu.make_async_copy(best_i, best_v, sem.at[0]),
-        pltpu.make_async_copy(cent_i, cent_v, sem.at[1]),
+def hand_on(best_i, cent_i, best_o, cent_o, sem):
+    copies = [
+        pltpu.make_async_copy(best_i, best_o, sem.at[0]),
+        pltpu.make_async_copy(cent_i, cent_o, sem.at[1]),
     ]
-    for copy in first:
+    for copy in copies:
         copy.start()
-    second = [
-        pltpu.make_async_copy(best_v, best_o, sem.at[2]),
-        pltpu.make_async_copy(cent_v, cent_o, sem.at[3]),
-    ]
-    for before, after in zip(first, second):
-        before.wait()
-        after.start()
-    for copy in second:
+    for copy in copies:
         copy.wait()
 
 
@@ -423,17 +435,18 @@
             pltpu.SemaphoreType.REGULAR, dma((8,)),
         ],
         compiler_params=pltpu.CompilerParams(
-            collective_id=0, has_side_effects=True, vmem_limit_bytes=56 << 20
+            collective_id=0, has_side_effects=True, vmem_limit_bytes=28 << 20
         ),
         name="semdedup_round",
-    )(
+    )(*[
+        pltpu.with_memory_space_constraint(a, pltpu.HBM) for a in (
         arrivals,
         home_owner.reshape(1, rows),
         cluster_slot.reshape(1, rows),
         bank.reshape(clusters * depth, width),
         members,
         centroid_sum,
-    )
+    )])
     best, cent = pl.pallas_call(
         hand_on,
         out_shape=(
@@ -441,7 +454,8 @@
         ),
         in_specs=[hbm, hbm],
         out_specs=(hbm, hbm),
-        scratch_shapes=[pltpu.VMEM(best.shape, F32), pltpu.VMEM(cent.shape, F32), dma((4,))],
+        scratch_shapes=[dma((2,))],
+        compiler_params=pltpu.CompilerParams(vmem_limit_bytes=4 << 20),
         name="hand_on",
     )(best, cent)
     return best.reshape(rows), cent.reshape(clusters, width)

time: 56 us -> 53.4 us (0.954)
  Pallas kernels: 55.2 us -> 52.6 us
    pallas_call x1, Pallas kernels: 53.3 us -> 51.8 us  [body(): pl.pallas_call(kernel, out_shape=(jax.ShapeDtypeStruct((1, rows), F32), j...]
    pallas_call x1, Pallas kernels: 1.87 us -> 0.82 us  [body(): pl.pallas_call(hand_on, out_shape=(jax.ShapeDtypeStruct(best.shape, F32),...]
where the time goes in v5:
time: 53.4 us; the launch traced here: 53.3 us
  Pallas kernels  52.6 us (99%)
  between operations  0.64 us (1%)
    pallas_call x1, Pallas kernels, body(): pl.pallas_call(kernel, out_shape=(jax.ShapeDtypeStruct((1, rows), F32), j...  51.8 us

profile of v5, /device:TPU:8, one launch (start us, length us, event | category | flops | bytes accessed | tf_op | source)
XLA Modules:
  0.0 53.3 jit_solution(7261862390866276488)
XLA Ops:
  0.6 51.8 %semdedup_round.1 = (f32[1,512]{1,0:T(1,128)S(1)}, f32[4,2,32,512]{3,2,1,0:T(8,128)S(1)}) custom-call(bf16[512,512]{1,0:T(8,128)(2,1)} %arr_h.1, s32[1,512]{1,0:T(1,128)} %bitcast.6, s32[1,512]{1,0:T(1,128)} %bitcast.7, bf16[8192,512]{1,0:T(8,128)(2,1)} %bitcast.5, s32[256]{0:T(256)} %mem_h.1, f32[256,512]{1,0:T(8,128)} %csum_h.1), custom_call_target="tpu_custom_call" | custom-call | tf_op jit(solution)/shard_map/semdedup_round/pallas_call | solution.py:401
  52.4 0.8 %hand_on.1 = (f32[1,512]{1,0:T(1,128)}, f32[4,2,32,512]{3,2,1,0:T(8,128)}) custom-call(f32[1,512]{1,0:T(1,128)S(1)} %get-tuple-element.6.best_i, f32[4,2,32,512]{3,2,1,0:T(8,128)S(1)} %get-tuple-element.7.cent_i), custom_call_target="tpu_custom_call" | custom-call | tf_op jit(solution)/shard_map/hand_on/pallas_call | solution.py:450

commit v6 on v5

--- a/solution.py
+++ b/solution.py
@@ -34,7 +34,7 @@
     tgt, slot, mem, arr, bank, rn, colc, kbuf, send, recv, scode, zcode, rcode, bests, ret, r8,
     acc, csum, passed, onward, partial, ag,
     in_sem, bank_sem, self_sem, row_ss, row_rs, code_ss, code_rs, ret_ss, ret_rs,
-    rs_ss, rs_rs, ag_ss, ag_rs, met, out_sem,
+    rs_ss, rs_rs, ag_ss, ag_rs, met,
 ):
     g = lax.axis_index("grp")
     me = lax.axis_index("own")
@@ -320,16 +320,14 @@
 
     def publish(far, half):
         at = lax.rem(g + far, 4)
-        return pltpu.make_async_copy(
-            ag.at[at, half], cent_o.at[at, half], out_sem.at[far * 2 + half]
-        )
+        cent_o[at, half] = ag[at, half]
 
     def spread_mine(step):
         for side in range(2):
             half = ag.at[g, side if step == 0 else 1 - side]
             to_next(half, half, ag_ss, ag_rs, step, side).start()
             if step == 0:
-                publish(0, side).start()
+                publish(0, side)
 
     spread_mine(0)
 
@@ -341,7 +339,7 @@
         half = ag.at[lax.rem(g + 3 + 2 * side, 4), side]
         to_next(half, half, ag_ss, ag_rs, 0, side).wait_recv()
         to_next(half, half, ag_ss, ag_rs, 2, side).start()
-        publish(3 if side == 0 else 1, side).start()
+        publish(3 if side == 0 else 1, side)
 
     for zi in range(8):
         landed(ret, zi, ret_rs).wait_recv()
@@ -362,10 +360,7 @@
         for step, far, half in ((1, 3 - 2 * side, 1 - side), (2, 2, side)):
             landing = ag.at[lax.rem(g + far, 4), half]
             to_next(landing, landing, ag_ss, ag_rs, step, side).wait_recv()
-            publish(far, half).start()
-    for far in range(4):
-        for half in range(2):
-            publish(far, half).wait()
+            publish(far, half)
 
     for zi in range(8):
         landed(send, zi, row_ss).wait_send()
@@ -405,7 +400,7 @@
             jax.ShapeDtypeStruct((4, 2, clusters // 8, width), F32),
         ),
         in_specs=[hbm] * 6,
-        out_specs=(vmem, hbm),
+        out_specs=(vmem, vmem),
         scratch_shapes=[
             pltpu.VMEM((1, rows), jnp.int32),
             pltpu.VMEM((1, rows), jnp.int32),
@@ -432,7 +427,7 @@
             dma((5,)), dma, dma,
             dma((8,)), dma((8,)), dma((8,)), dma((8,)), dma((8,)), dma((8,)),
             dma((6,)), dma((6,)), dma((6,)), dma((6,)),
-            pltpu.SemaphoreType.REGULAR, dma((8,)),
+            pltpu.SemaphoreType.REGULAR,
         ],
         compiler_params=pltpu.CompilerParams(
             collective_id=0, has_side_effects=True, vmem_limit_bytes=28 << 20

time: 53.4 us -> 53.1 us (level)
  no operation moved by 1% of the time
where the time goes in v6:
time: 53.1 us; the launch traced here: 53 us
  Pallas kernels  52.3 us (98%)
  between operations  0.64 us (1%)
    pallas_call x1, Pallas kernels, body(): pl.pallas_call(kernel, out_shape=(jax.ShapeDtypeStruct((1, rows), F32), j...  51.5 us

profile of v6, /device:TPU:8, one launch (start us, length us, event | category | flops | bytes accessed | tf_op | source)
XLA Modules:
  0.0 53.0 jit_solution(14580912368027360114)
XLA Ops:
  0.6 51.5 %semdedup_round.1 = (f32[1,512]{1,0:T(1,128)S(1)}, f32[4,2,32,512]{3,2,1,0:T(8,128)S(1)}) custom-call(bf16[512,512]{1,0:T(8,128)(2,1)} %arr_h.1, s32[1,512]{1,0:T(1,128)} %bitcast.6, s32[1,512]{1,0:T(1,128)} %bitcast.7, bf16[8192,512]{1,0:T(8,128)(2,1)} %bitcast.5, s32[256]{0:T(256)} %mem_h.1, f32[256,512]{1,0:T(8,128)} %csum_h.1), custom_call_target="tpu_custom_call" | custom-call | tf_op jit(solution)/shard_map/semdedup_round/pallas_call | solution.py:396
  52.2 0.8 %hand_on.1 = (f32[1,512]{1,0:T(1,128)}, f32[4,2,32,512]{3,2,1,0:T(8,128)}) custom-call(f32[1,512]{1,0:T(1,128)S(1)} %get-tuple-element.6.best_i, f32[4,2,32,512]{3,2,1,0:T(8,128)S(1)} %get-tuple-element.7.cent_i), custom_call_target="tpu_custom_call" | custom-call | tf_op jit(solution)/shard_map/hand_on/pallas_call | solution.py:445

commit v7 on v6

--- a/solution.py
+++ b/solution.py
@@ -14,7 +14,7 @@
 SELF_GROUP = Z_ORDER.index(0)
 F32, BF16 = jnp.float32, jnp.bfloat16
 TILE = 2048
-FACTOR, DEFER = 1, 1
+FACTOR, DEFER = 2, 2
 
 
 def nt(a, b):

time: 53.1 us -> 53 us (level)
  no operation moved by 1% of the time
where the time goes in v7:
time: 53 us; the launch traced here: 52.9 us
  Pallas kernels  52.3 us (99%)
  between operations  0.64 us (1%)
    pallas_call x1, Pallas kernels, body(): pl.pallas_call(kernel, out_shape=(jax.ShapeDtypeStruct((1, rows), F32), j...  51.4 us

profile of v7, /device:TPU:8, one launch (start us, length us, event | category | flops | bytes accessed | tf_op | source)
XLA Modules:
  0.0 52.9 jit_solution(9689859686606659584)
XLA Ops:
  0.6 51.4 %semdedup_round.1 = (f32[1,512]{1,0:T(1,128)S(1)}, f32[4,2,32,512]{3,2,1,0:T(8,128)S(1)}) custom-call(bf16[512,512]{1,0:T(8,128)(2,1)} %arr_h.1, s32[1,512]{1,0:T(1,128)} %bitcast.6, s32[1,512]{1,0:T(1,128)} %bitcast.7, bf16[8192,512]{1,0:T(8,128)(2,1)} %bitcast.5, s32[256]{0:T(256)} %mem_h.1, f32[256,512]{1,0:T(8,128)} %csum_h.1), custom_call_target="tpu_custom_call" | custom-call | tf_op jit(solution)/shard_map/semdedup_round/pallas_call | solution.py:396
  52.1 0.8 %hand_on.1 = (f32[1,512]{1,0:T(1,128)}, f32[4,2,32,512]{3,2,1,0:T(8,128)}) custom-call(f32[1,512]{1,0:T(1,128)S(1)} %get-tuple-element.6.best_i, f32[4,2,32,512]{3,2,1,0:T(8,128)S(1)} %get-tuple-element.7.cent_i), custom_call_target="tpu_custom_call" | custom-call | tf_op jit(solution)/shard_map/hand_on/pallas_call | solution.py:445
